TPU v7x, 32 devices: a whole 2x2x4 slice. The times are simulated.
32 devices in a mesh: groups: 2 (over x), rows: 16 (over z, y, core).
Axes of the slice: x: 2, y: 2, z: 4, core: 2. Of those that a mesh axis runs over, the one named last changes fastest.
Arguments:
- volume: bfloat16 [32, 128, 8, 512], P(None, ('groups', 'rows')), parts along dimension 1, may hold values from -6 to 6
- fine_first: bfloat16 [3, 3, 3, 32, 32], replicated, may hold values from -0.3125 to 0.3125
- fine_second: bfloat16 [3, 3, 3, 32, 32], replicated, may hold values from -0.3125 to 0.3125
- middle_first: bfloat16 [3, 3, 3, 64, 32], replicated, may hold values from -0.3125 to 0.3125
- middle_second: bfloat16 [3, 3, 3, 64, 64], replicated, may hold values from -0.21875 to 0.21875
- bottom_first: bfloat16 [3, 3, 3, 256, 64], P(None, None, None, 'rows'), may hold values from -0.21875 to 0.21875
- bottom_second: bfloat16 [3, 3, 3, 256, 256], P(None, None, None, 'rows'), may hold values from -0.109375 to 0.109375
- upsample_bottom: bfloat16 [2, 2, 2, 64, 256], replicated, may hold values from -1.5 to 1.5
- middle_merge: bfloat16 [3, 3, 3, 64, 128], replicated, may hold values from -0.078125 to 0.078125
- middle_refine: bfloat16 [3, 3, 3, 64, 64], replicated, may hold values from -0.21875 to 0.21875
- upsample_middle: bfloat16 [2, 2, 2, 32, 64], replicated, may hold values from -1.5 to 1.5
- fine_merge: bfloat16 [3, 3, 3, 32, 64], replicated, may hold values from -0.109375 to 0.109375
- fine_refine: bfloat16 [3, 3, 3, 32, 32], replicated, may hold values from -0.3125 to 0.3125
Outputs:
- decoded: bfloat16 [32, 128, 8, 512], P(None, ('groups', 'rows')), parts along dimension 1
There are 2 independent parts, one for each index of `groups`. A program takes and returns all parts, laid end to end along the dimension named above; an argument that names none is the same for every part. Nothing has to cross between parts.
All inputs are finite; a program needn't handle non-finite values.
Results may differ from a plain program's by a relative error of at most 0.02.
Values may be sent and summed in bfloat16 or wider, within the bound.
A program may use at most 128 MiB of HBM per device.

v0:
```python
import functools

import jax
import jax.numpy as jnp
from jax import lax
from jax.experimental import pallas as pl
from jax.experimental.pallas import tpu as pltpu
from jax.sharding import PartitionSpec as P

leakage = 0.01
bf16, f32 = jnp.bfloat16, jnp.float32
VMEM_LIMIT = 56 * 2**20


def iota(shape, axis):
    return lax.broadcasted_iota(jnp.int32, shape, axis)


def one_hot(mask):
    return jnp.where(mask, 1.0, 0.0).astype(bf16)


def dot(a, b):
    return jnp.dot(a, b, preferred_element_type=f32)


def spread(total, channels, offset, copies):
    shape = (total, copies * channels)
    return one_hot((iota(shape, 1) & (channels - 1)) + offset == iota(shape, 0))


def band(target, tap, outs, ins, depth):
    block = iota((outs, depth * ins), 1) // ins
    zero = jnp.zeros((outs, depth * ins), f32)
    for a in range(3):
        for c in range(3):
            taps = [tap(a, b, c) for b in range(3)]
            for z in range(depth):
                rows = zero
                for b in range(3):
                    if 0 <= z + b - 1 < depth:
                        rows = jnp.where(block == z + b - 1, taps[b], rows)
                start = (c * depth + z) * outs
                target[start : start + outs, a * depth * ins : (a + 1) * depth * ins] = rows.astype(bf16)


def band_kernel(target, kernel_ref, outs, total, ins, offset, depth):
    picks = spread(total, ins, offset, depth)

    def tap(a, b, c):
        at = ((a * 3 + b) * 3 + c) * outs
        return dot(kernel_ref[at : at + outs, :], picks)

    band(target, tap, outs, ins, depth)


def finish(sums, count):
    width = sums.shape[1]
    lane = iota((count, width), 1)
    left = jnp.where(lane == 0, 0.0, pltpu.roll(sums[:count], 1, 1))
    right = jnp.where(lane == width - 1, 0.0, pltpu.roll(sums[2 * count :], width - 1, 1))
    total = left + sums[count : 2 * count] + right
    return jnp.maximum(total, leakage * total).astype(bf16)


def conv_rows(sources, store, height, count, arrive):
    def row(at):
        sums = None
        for banded, rows, cells in sources:
            part = dot(banded[...], rows[pl.ds(pl.multiple_of(at * cells, cells), 3 * cells), :])
            sums = part if sums is None else sums + part
        store(at, finish(sums, count))

    if height > 2:

        @pl.loop(1, height - 1)
        def _(at):
            row(at)

    arrive()
    if height == 1:
        row(0)
    else:

        @pl.loop(0, 2)
        def _(end):
            row(end * (height - 1))


class Edges:
    def __init__(self, groups, rows, count, send, recv):
        self.group, self.me, self.count = lax.axis_index(groups), lax.axis_index(rows), count
        self.send, self.recv = send, recv

    def greet(self):
        barrier = pltpu.get_barrier_semaphore()

        @pl.when(self.me > 0)
        def _():
            pl.semaphore_signal(barrier, inc=1, device_id=(self.group, self.me - 1), device_id_type=pl.DeviceIdType.MESH)

        @pl.when(self.me < self.count - 1)
        def _():
            pl.semaphore_signal(barrier, inc=1, device_id=(self.group, self.me + 1), device_id_type=pl.DeviceIdType.MESH)

        inner = (self.me > 0) & (self.me < self.count - 1)

        @pl.when(inner)
        def _():
            pl.semaphore_wait(barrier, 2)

        @pl.when(jnp.logical_not(inner))
        def _():
            pl.semaphore_wait(barrier, 1)

    def copies(self, buf, height, cells, at):
        def one(source, target, way, step):
            return pltpu.make_async_remote_copy(
                src_ref=buf.at[pl.ds(source * cells, cells)],
                dst_ref=buf.at[pl.ds(target * cells, cells)],
                send_sem=self.send.at[at, way],
                recv_sem=self.recv.at[at, way],
                device_id=(self.group, self.me + step),
                device_id_type=pl.DeviceIdType.MESH,
            )

        return one(1, height + 1, 0, -1), one(height, 0, 1, 1)

    def start(self, buf, height, cells, at):
        up, down = self.copies(buf, height, cells, at)

        @pl.when(self.me > 0)
        def _():
            up.start()

        @pl.when(self.me < self.count - 1)
        def _():
            down.start()

    def arrive(self, buf, height, cells, at):
        up, down = self.copies(buf, height, cells, at)
        zero = jnp.zeros((cells, buf.shape[1]), bf16)

        @pl.when(self.me < self.count - 1)
        def _():
            up.wait_recv()

        @pl.when(self.me == self.count - 1)
        def _():
            buf[(height + 1) * cells : (height + 2) * cells, :] = zero

        @pl.when(self.me > 0)
        def _():
            down.wait_recv()

        @pl.when(self.me == 0)
        def _():
            buf[0:cells, :] = zero

    def sent(self, buf, height, cells, at):
        up, down = self.copies(buf, height, cells, at)

        @pl.when(self.me > 0)
        def _():
            up.wait_send()

        @pl.when(self.me < self.count - 1)
        def _():
            down.wait_send()


def into(buf, cells):
    def store(at, value):
        buf[pl.ds(pl.multiple_of((at + 1) * cells, cells), cells), :] = value

    return store


def plain(buf, cells):
    def store(at, value):
        buf[pl.ds(pl.multiple_of(at * cells, cells), cells), :] = value

    return store


def halves(width):
    half = width // 2
    source, target = iota((width, width), 0), iota((width, width), 1)
    return one_hot(source == jnp.where(target < half, 2 * target, 2 * (target - half) + 1))


def weave(width):
    half = width // 2
    source, target = iota((width, width), 0), iota((width, width), 1)
    return one_hot(target == jnp.where(source < half, 2 * source, 2 * (source - half) + 1))


def pool(first, second, chans, parts):
    rows = jnp.maximum(first, second)
    depth, width = rows.shape[0] // chans, rows.shape[1]
    pairs = [
        jnp.maximum(rows[z * chans : (z + 1) * chans], rows[(z + 1) * chans : (z + 2) * chans])
        for z in range(0, depth, 2)
    ]
    split = dot(jnp.concatenate(pairs, axis=0), parts)
    return jnp.maximum(split[:, : width // 2], split[:, width // 2 :]).astype(bf16)


def lift(rows, kernel_ref, ins, outs, woven, store):
    depth = rows.shape[0] // ins
    parts = [dot(kernel_ref[...], rows[z * ins : (z + 1) * ins]).astype(bf16) for z in range(depth)]
    for a in range(2):
        stack = []
        for z in range(depth):
            for b in range(2):
                at = (a * 2 + b) * 2 * outs
                stack.append(jnp.concatenate([parts[z][at : at + outs], parts[z][at + outs : at + 2 * outs]], axis=1))
        store(a, dot(jnp.concatenate(stack, axis=0), woven).astype(bf16))


def encoder(size, groups, rows, count, *refs):
    (vol, k1, k2, k3, k4, fine_out, mid_out, low_out) = refs[:8]
    (b_vol, b_one, b_pool, b_mid, t1, t2, t3, t4, send, recv, local) = refs[8:]
    H, Z, W, C1, C2 = size
    R, R2, RP = Z * C1, Z // 2 * C2, Z // 2 * C1
    edges = Edges(groups, rows, count, send, recv)
    load = pltpu.make_async_copy(vol, b_vol.at[pl.ds(R, H * R)], local)
    load.start()
    edges.greet()
    load.wait()
    edges.start(b_vol, H, R, 0)
    band_kernel(t1, k1, C1, C1, C1, 0, Z)
    conv_rows([(t1, b_vol, R)], into(b_one, R), H, R, lambda: edges.arrive(b_vol, H, R, 0))
    edges.start(b_one, H, R, 1)
    band_kernel(t2, k2, C1, C1, C1, 0, Z)
    conv_rows([(t2, b_one, R)], plain(fine_out, R), H, R, lambda: edges.arrive(b_one, H, R, 1))
    parts = halves(W)
    for h in range(H // 2):
        first, second = fine_out[2 * h * R : (2 * h + 1) * R, :], fine_out[(2 * h + 1) * R : (2 * h + 2) * R, :]
        b_pool[(h + 1) * RP : (h + 2) * RP, :] = pool(first, second, C1, parts)
    edges.start(b_pool, H // 2, RP, 2)
    band_kernel(t3, k3, C2, C1, C1, 0, Z // 2)
    conv_rows([(t3, b_pool, RP)], into(b_mid, R2), H // 2, R2, lambda: edges.arrive(b_pool, H // 2, RP, 2))
    edges.start(b_mid, H // 2, R2, 3)
    band_kernel(t4, k4, C2, C2, C2, 0, Z // 2)
    conv_rows([(t4, b_mid, R2)], plain(mid_out, R2), H // 2, R2, lambda: edges.arrive(b_mid, H // 2, R2, 3))
    parts = halves(W // 2)
    R3 = R2 // 2
    for h in range(H // 4):
        first, second = mid_out[2 * h * R2 : (2 * h + 1) * R2, :], mid_out[(2 * h + 1) * R2 : (2 * h + 2) * R2, :]
        low_out[h * R3 : (h + 1) * R3, :] = pool(first, second, C2, parts)
    edges.sent(b_vol, H, R, 0)
    edges.sent(b_one, H, R, 1)
    edges.sent(b_pool, H // 2, RP, 2)
    edges.sent(b_mid, H // 2, R2, 3)


def decoder(size, groups, rows, count, *refs):
    (fine, mid, low, whole, ub, mm, mr, um, fm, fr, out) = refs[:11]
    (b_fine, b_mid, b_low, b_bot, bot, b_lift, b_three, four, b_raise, b_last) = refs[11:21]
    (kt, t1, t2, t3a, t3b, t4, t5a, t5b, t6, send, recv, local) = refs[21:]
    H, Z, W, C1, C2, C3 = size
    R, R2, RP, RB = Z * C1, Z // 2 * C2, Z // 4 * C2, Z // 4 * C3
    H2, H4 = H // 2, H // 4
    edges = Edges(groups, rows, count, send, recv)
    loads = [
        pltpu.make_async_copy(low, b_low.at[pl.ds(RP, H4 * RP)], local.at[0]),
        pltpu.make_async_copy(mid, b_mid.at[pl.ds(R2, H2 * R2)], local.at[1]),
        pltpu.make_async_copy(fine, b_fine.at[pl.ds(R, H * R)], local.at[2]),
    ]
    for load in loads:
        load.start()
    edges.greet()
    loads[0].wait()
    edges.start(b_low, H4, RP, 0)
    loads[1].wait()
    edges.start(b_mid, H2, R2, 1)
    loads[2].wait()
    edges.start(b_fine, H, R, 2)
    side = C3 // C2
    each = -(-27 // side)
    wide = Z // 4 * C2
    shape = (C3, side * wide)
    picks = one_hot(iota(shape, 0) == iota(shape, 1) // wide * C2 + (iota(shape, 1) & (C2 - 1)))
    for t in range(each):
        taps = dot(whole[:, 27 + t].reshape(C3, C3), picks).astype(bf16)
        for q in range(side):
            if q * each + t < 27:
                at = (q * each + t) * C3
                kt[at : at + C3, :] = taps[:, q * wide : (q + 1) * wide]

    def tap(a, b, c):
        at = ((a * 3 + b) * 3 + c) * C3
        return kt[at : at + C3, :].astype(f32)

    band(t1, tap, C3, C2, Z // 4)
    conv_rows([(t1, b_low, RP)], into(b_bot, RB), H4, RB, lambda: edges.arrive(b_low, H4, RP, 0))
    edges.start(b_bot, H4, RB, 3)
    for a in range(3):
        for c in range(3):
            for z in range(Z // 4):
                for y in range(Z // 4):
                    r, l = (c * (Z // 4) + z) * C3, (a * (Z // 4) + y) * C3
                    if -1 <= y - z <= 1:
                        t2[r : r + C3, l : l + C3] = whole[:, (a * 3 + y - z + 1) * 3 + c].reshape(C3, C3)
                    else:
                        t2[r : r + C3, l : l + C3] = jnp.zeros((C3, C3), bf16)
    conv_rows([(t2, b_bot, RB)], plain(bot, RB), H4, RB, lambda: edges.arrive(b_bot, H4, RB, 3))
    woven = weave(W // 2)
    for h in range(H4):

        def store(a, value):
            at = (2 * h + a + 1) * R2
            b_lift[at : at + R2, :] = value

        lift(bot[h * RB : (h + 1) * RB, :], ub, C3, C2, woven, store)
    edges.start(b_lift, H2, R2, 4)
    band_kernel(t3a, mm, C2, 2 * C2, C2, 0, Z // 2)
    band_kernel(t3b, mm, C2, 2 * C2, C2, C2, Z // 2)

    def both():
        edges.arrive(b_mid, H2, R2, 1)
        edges.arrive(b_lift, H2, R2, 4)

    conv_rows([(t3a, b_mid, R2), (t3b, b_lift, R2)], into(b_three, R2), H2, R2, both)
    edges.start(b_three, H2, R2, 5)
    band_kernel(t4, mr, C2, C2, C2, 0, Z // 2)
    conv_rows([(t4, b_three, R2)], plain(four, R2), H2, R2, lambda: edges.arrive(b_three, H2, R2, 5))
    woven = weave(W)
    for h in range(H2):

        def store(a, value):
            at = (2 * h + a + 1) * R
            b_raise[at : at + R, :] = value

        lift(four[h * R2 : (h + 1) * R2, :], um, C2, C1, woven, store)
    edges.start(b_raise, H, R, 6)
    band_kernel(t5a, fm, C1, 2 * C1, C1, 0, Z)
    band_kernel(t5b, fm, C1, 2 * C1, C1, C1, Z)

    def last():
        edges.arrive(b_fine, H, R, 2)
        edges.arrive(b_raise, H, R, 6)

    conv_rows([(t5a, b_fine, R), (t5b, b_raise, R)], into(b_last, R), H, R, last)
    edges.start(b_last, H, R, 7)
    band_kernel(t6, fr, C1, C1, C1, 0, Z)
    conv_rows([(t6, b_last, R)], plain(out, R), H, R, lambda: edges.arrive(b_last, H, R, 7))
    for at, (buf, height, cells) in enumerate(
        [(b_low, H4, RP), (b_mid, H2, R2), (b_fine, H, R), (b_bot, H4, RB), (b_lift, H2, R2), (b_three, H2, R2), (b_raise, H, R), (b_last, H, R)]
    ):
        edges.sent(buf, height, cells, at)


def per_device(count, *args):
    (volume, f1, f2, m1, m2, b1, b2, ub, mm, mr, um, fm, fr) = args
    C1, H, Z, W = volume.shape
    C2, C3 = m1.shape[3], b2.shape[4]
    own = b1.shape[3]
    R, R2, RP, RL, RB = Z * C1, Z // 2 * C2, Z // 2 * C1, Z // 4 * C2, Z // 4 * C3
    H2, H4, W2, W4 = H // 2, H // 4, W // 2, W // 4
    flat = lambda k: k.reshape(-1, k.shape[-1])
    side = C3 // C2
    each = -(-27 // side)
    first = jnp.pad(b1.reshape(27, own, C2), ((0, each * side - 27), (0, 0), (0, 0))).reshape(side, each, own, C2)
    first = jnp.concatenate([first[q] for q in range(side)], axis=-1)
    packed = jnp.concatenate([b2.reshape(27, own, C3), first], axis=0)
    whole = lax.all_gather(packed, "rows", axis=0)
    cells = volume.transpose(1, 2, 0, 3).reshape(H * R, W)
    vmem, hbm = pl.BlockSpec(memory_space=pltpu.VMEM), pl.BlockSpec(memory_space=pl.ANY)
    V = lambda r, c: pltpu.VMEM((r, c), bf16)
    D = pltpu.SemaphoreType.DMA
    fine, mid, low = pl.pallas_call(
        functools.partial(encoder, (H, Z, W, C1, C2), "groups", "rows", count),
        out_shape=[jax.ShapeDtypeStruct(s, bf16) for s in ((H * R, W), (H2 * R2, W2), (H4 * RL, W4))],
        in_specs=[hbm] + [vmem] * 4,
        out_specs=[vmem] * 3,
        scratch_shapes=[
            V((H + 2) * R, W), V((H + 2) * R, W), V((H2 + 2) * RP, W2), V((H2 + 2) * R2, W2),
            V(3 * R, 3 * R), V(3 * R, 3 * R), V(3 * R2, 3 * RP), V(3 * R2, 3 * R2),
            D((4, 2)), D((4, 2)), D,
        ],
        compiler_params=pltpu.CompilerParams(collective_id=0, has_side_effects=True, vmem_limit_bytes=VMEM_LIMIT),
        cost_estimate=pl.CostEstimate(flops=10**10, bytes_accessed=10**8, transcendentals=0),
        name="encoder",
    )(cells, flat(f1), flat(f2), flat(m1), flat(m2))
    out = pl.pallas_call(
        functools.partial(decoder, (H, Z, W, C1, C2, C3), "groups", "rows", count),
        out_shape=jax.ShapeDtypeStruct((H * R, W), bf16),
        in_specs=[hbm] * 3 + [vmem] * 7,
        out_specs=vmem,
        scratch_shapes=[
            V((H + 2) * R, W), V((H2 + 2) * R2, W2), V((H4 + 2) * RL, W4), V((H4 + 2) * RB, W4), V(H4 * RB, W4),
            V((H2 + 2) * R2, W2), V((H2 + 2) * R2, W2), V(H2 * R2, W2), V((H + 2) * R, W), V((H + 2) * R, W),
            V(27 * C3, Z // 4 * C2), V(3 * RB, 3 * RL), V(3 * RB, 3 * RB), V(3 * R2, 3 * R2), V(3 * R2, 3 * R2),
            V(3 * R2, 3 * R2), V(3 * R, 3 * R), V(3 * R, 3 * R), V(3 * R, 3 * R),
            D((8, 2)), D((8, 2)), D((3,)),
        ],
        compiler_params=pltpu.CompilerParams(collective_id=1, has_side_effects=True, vmem_limit_bytes=VMEM_LIMIT),
        cost_estimate=pl.CostEstimate(flops=10**10, bytes_accessed=10**8, transcendentals=0),
        name="decoder",
    )(fine, mid, low, whole, flat(ub), flat(mm), flat(mr), flat(um), flat(fm), flat(fr))
    return out.reshape(H, Z, C1, W).transpose(2, 0, 1, 3)


def solution(mesh):
    placed = [P(None, ("groups", "rows"), None, None)] + [P()] * 12
    placed[5] = placed[6] = P(None, None, None, "rows", None)
    return jax.shard_map(
        functools.partial(per_device, mesh.shape["rows"]),
        mesh=mesh,
        in_specs=tuple(placed),
        out_specs=P(None, ("groups", "rows"), None, None),
        check_vma=False,
    )
```

profile of v0, /device:TPU:9, one launch (start us, length us, event | category | flops | bytes accessed | tf_op | source)
XLA Modules:
  0.0 126.2 jit_solution(15603354958475626869)
XLA Ops:
  6.5 0.0 all-gather.3.cloned.1.call-start
  6.5 0.8 fusion
  7.3 1.8 %maximum_maximum_fusion = bf16[34,16,256]{2,1,0:T(8,128)(2,1)} fusion(bf16[7,16,64]{2,1,0:T(8,128)(2,1)S(1)} %get-tuple-element.12, bf16[7,16,64]{2,1,0:T(8,128)(2,1)S(1)} %get-tuple-element.13, bf16[7,16,64]{2,1,0:T(8,128)(2,1)S(1)} %get-tuple-element.14, bf16[7,16,64]{2,1,0:T(8,128)(2,1)S(1)} %get-tuple-element.11, bf16[27,16,256]{2,1,0:T(8,128)(2,1)} %bitcast.24), kind=kLoop, calls=%fused_computation.1 | loop fusion | flops 1392640 | bytes 557056 | tf_op jit(solution)/shard_map/concatenate | solution.py:367
  9.1 0.0 all-gather.3.cloned.1.call-update
  9.1 2.8 %copy.17 = bf16[4,8,32,512]{3,2,1,0:T(8,128)(2,1)} copy(bf16[4,8,32,512]{3,1,0,2:T(8,128)(2,1)} %bitcast.19) | data formatting | bytes 2097152 | tf_op jit(solution)/shard_map/transpose | solution.py:369
  11.9 1.9 %copy.18 = bf16[3,3,3,64,32]{4,3,2,1,0:T(8,128)(2,1)} copy(bf16[3,3,3,64,32]{3,4,2,1,0:T(8,128)(2,1)} %param.16) | data formatting | bytes 221184 | tf_op args[3]
  13.8 38.8 %encoder.1 = (bf16[1024,512]{1,0:T(8,128)(2,1)}, bf16[512,256]{1,0:T(8,128)(2,1)}, bf16[128,128]{1,0:T(8,128)(2,1)}) custom-call(bf16[1024,512]{1,0:T(8,128)(2,1)} %bitcast.20, bf16[864,32]{1,0:T(8,128)(2,1)} %bitcast.30, bf16[864,32]{1,0:T(8,128)(2,1)} %bitcast.31, bf16[1728,32]{1,0:T(8,128)(2,1)} %bitcast.22, bf16[1728,64]{1,0:T(8,128)(2,1)} %bitcast.26), custom_call_target="tpu_custom_call" | custom-call | flops 10000000000 | bytes 100000000 | tf_op jit(solution)/shard_map/encoder/pallas_call | solution.py:373
  52.6 14.5 %all-gather.3.cloned.1.call-done = bf16[544,16,256]{2,1,0:T(8,128)(2,1)} async-done(((bf16[34,16,256]{2,1,0:T(8,128)(2,1)}), bf16[544,16,256]{2,1,0:T(8,128)(2,1)}) %all-gather.3.cloned.1.call-update) | async-done | bytes 4456464 | tf_op jit(solution)/shard_map/all_gather | solution.py:368
  67.1 49.5 %decoder.1 = bf16[1024,512]{1,0:T(8,128)(2,1)} custom-call(bf16[1024,512]{1,0:T(8,128)(2,1)} %get-tuple-element.8.refs_0_, bf16[512,256]{1,0:T(8,128)(2,1)} %get-tuple-element.9.refs_1_, bf16[128,128]{1,0:T(8,128)(2,1)} %get-tuple-element.10.refs_2_, bf16[16,34,16,256]{3,2,1,0:T(8,128)(2,1)} %bitcast.25, bf16[512,256]{1,0:T(8,128)(2,1)} %bitcast.29, ...), custom_call_target="tpu_custom_call" | custom-call | flops 10000000000 | bytes 100000000 | tf_op jit(solution)/shard_map/decoder/pallas_call | solution.py:387
  116.6 2.8 %copy.21 = bf16[4,8,32,512]{3,1,0,2:T(8,128)(2,1)} copy(bf16[4,8,32,512]{3,2,1,0:T(8,128)(2,1)} %bitcast.21) | data formatting | bytes 2097152 | tf_op jit(solution)/shard_map/reshape | solution.py:403
Async XLA Ops:
  6.5 60.6 %all-gather.3.cloned.1.call-start = ((), (), s32[]{:S(2)}) async-start(), calls=%async_computation | async-start | bytes 4734976 | tf_op jit(solution)/shard_map/all_gather | solution.py:368
Sparse Core Ops, SparseCore 0:
  9.6 57.4 all-gather.2
where the time goes:
time: 128 us; the launch traced here: 126 us
  Pallas kernels  88.2 us (69%)
  waiting for transfers between devices  14.5 us (11%)
  between operations  13.4 us (10%)
  local copies, waits for them, and re-layouts  8.27 us (6%)
  other arithmetic  1.76 us (1%)
    pallas_call x1, Pallas kernels, per_device(): pl.pallas_call(functools.partial(decoder, (H, Z, W, C1, C2, C3), 'groups'...  49.5 us
    pallas_call x1, Pallas kernels, per_device(): pl.pallas_call(functools.partial(encoder, (H, Z, W, C1, C2), 'groups', 'r...  38.8 us
    all_gather x1, waiting for transfers between devices, per_device(): whole = lax.all_gather(packed, 'rows', axis=0)  14.5 us
    transpose x1, local copies, waits for them, and re-layouts, per_device(): cells = volume.transpose(1, 2, 0, 3).reshape(H * R, W)  2.77 us
    reshape x1, local copies, waits for them, and re-layouts, per_device(): return out.reshape(H, Z, C1, W).transpose(2, 0, 1, 3)  2.77 us
  transfers between devices with their start and end apart: 1, of which 1 were waited for; matrix products, arithmetic and copies ran while one was open for 4% of the time, Pallas kernels for 31%

commit v1 on v0

--- a/solution.py
+++ b/solution.py
@@ -44,12 +44,15 @@
                 target[start : start + outs, a * depth * ins : (a + 1) * depth * ins] = rows.astype(bf16)
 
 
-def band_kernel(target, kernel_ref, outs, total, ins, offset, depth):
+def band_kernel(target, kernel_ref, outs, total, ins, offset, depth, turned=False):
     picks = spread(total, ins, offset, depth)
 
     def tap(a, b, c):
-        at = ((a * 3 + b) * 3 + c) * outs
-        return dot(kernel_ref[at : at + outs, :], picks)
+        at = (a * 3 + b) * 3 + c
+        if turned:
+            block = kernel_ref[at * total : (at + 1) * total, :]
+            return lax.dot_general(block, picks, (((0,), (0,)), ((), ())), preferred_element_type=f32)
+        return dot(kernel_ref[at * outs : (at + 1) * outs, :], picks)
 
     band(target, tap, outs, ins, depth)
 
@@ -63,7 +66,7 @@
     return jnp.maximum(total, leakage * total).astype(bf16)
 
 
-def conv_rows(sources, store, height, count, arrive):
+def conv_rows(sources, store, height, count, arrive, before=lambda: None):
     def row(at):
         sums = None
         for banded, rows, cells in sources:
@@ -77,6 +80,7 @@
         def _(at):
             row(at)
 
+    before()
     arrive()
     if height == 1:
         row(0)
@@ -92,26 +96,32 @@
         self.group, self.me, self.count = lax.axis_index(groups), lax.axis_index(rows), count
         self.send, self.recv = send, recv
 
-    def greet(self):
+    def greet(self, others):
         barrier = pltpu.get_barrier_semaphore()
 
+        def signal(to):
+            pl.semaphore_signal(barrier, inc=1, device_id=(self.group, to), device_id_type=pl.DeviceIdType.MESH)
+
+        for other in others:
+            signal(other)
+
         @pl.when(self.me > 0)
         def _():
-            pl.semaphore_signal(barrier, inc=1, device_id=(self.group, self.me - 1), device_id_type=pl.DeviceIdType.MESH)
+            signal(self.me - 1)
 
         @pl.when(self.me < self.count - 1)
         def _():
-            pl.semaphore_signal(barrier, inc=1, device_id=(self.group, self.me + 1), device_id_type=pl.DeviceIdType.MESH)
+            signal(self.me + 1)
 
         inner = (self.me > 0) & (self.me < self.count - 1)
 
         @pl.when(inner)
         def _():
-            pl.semaphore_wait(barrier, 2)
+            pl.semaphore_wait(barrier, 2 + len(others))
 
         @pl.when(jnp.logical_not(inner))
         def _():
-            pl.semaphore_wait(barrier, 1)
+            pl.semaphore_wait(barrier, 1 + len(others))
 
     def copies(self, buf, height, cells, at):
         def one(source, target, way, step):
@@ -169,6 +179,88 @@
             down.wait_send()
 
 
+class Ring:
+    def __init__(self, edges, whole, send, recv, side_send, side_recv):
+        self.edges, self.whole = edges, whole
+        self.sems = send, recv, side_send, side_recv
+        self.chips = edges.count // 2
+        self.core = lax.rem(edges.me, 2)
+        chip = edges.me // 2
+        self.place = jnp.where(lax.rem(chip, 2) == 0, chip // 2, self.chips - 1 - chip // 2)
+        self.mate = edges.me + 1 - 2 * self.core
+        self.cut = whole.shape[1] // 2
+
+    def at(self, place):
+        place = lax.rem(place + 2 * self.chips, self.chips)
+        chip = jnp.where(place < self.chips // 2, 2 * place, 2 * (self.chips - 1 - place) + 1)
+        return 2 * chip + self.core
+
+    def neighbours(self):
+        return [self.at(self.place + 1), self.at(self.place - 1)]
+
+    def copy(self, slot, way, to, send, recv):
+        part = self.whole.at[slot, pl.ds(way * self.cut, self.cut)]
+        return pltpu.make_async_remote_copy(
+            src_ref=part,
+            dst_ref=part,
+            send_sem=send,
+            recv_sem=recv,
+            device_id=(self.edges.group, to),
+            device_id_type=pl.DeviceIdType.MESH,
+        )
+
+    def hop(self, step, way):
+        sign = 1 - 2 * way
+        send, recv = self.sems[0].at[step, way], self.sems[1].at[step, way]
+        return self.copy(self.at(self.place - sign * step), way, self.at(self.place + sign), send, recv)
+
+    def landed(self, step, way):
+        sign = 1 - 2 * way
+        send, recv = self.sems[0].at[step, way], self.sems[1].at[step, way]
+        return self.copy(self.at(self.place - sign * (step + 1)), way, self.at(self.place + sign), send, recv)
+
+    def across(self, step, way, other=False):
+        sign = 1 - 2 * way
+        slot = self.at(self.place - sign * (step + 1))
+        slot = slot + 1 - 2 * self.core if other else slot
+        return self.copy(slot, way, self.mate, self.sems[2].at[step + 1, way], self.sems[3].at[step + 1, way])
+
+    def step(self, at):
+        if isinstance(at, int) and at >= self.chips:
+            return
+        for way in range(2):
+            if not isinstance(at, int) or at > 0:
+                self.landed(at - 1, way).wait_recv()
+            if not isinstance(at, int) or at < self.chips - 1:
+                self.hop(at, way).start()
+            self.across(at - 1, way).start()
+
+    def finish(self, done):
+        if done < self.chips:
+
+            @pl.loop(done, self.chips - 1)
+            def _(at):
+                self.step(at)
+
+            self.step(self.chips - 1)
+
+        @pl.loop(0, self.chips)
+        def _(at):
+            for way in range(2):
+                self.across(at - 1, way, True).wait_recv()
+
+    def sent(self):
+        @pl.loop(0, self.chips)
+        def _(at):
+            for way in range(2):
+                self.across(at - 1, way).wait_send()
+
+        @pl.loop(0, self.chips - 1)
+        def _(at):
+            for way in range(2):
+                self.hop(at, way).wait_send()
+
+
 def into(buf, cells):
     def store(at, value):
         buf[pl.ds(pl.multiple_of((at + 1) * cells, cells), cells), :] = value
@@ -218,67 +310,60 @@
         store(a, dot(jnp.concatenate(stack, axis=0), woven).astype(bf16))
 
 
-def encoder(size, groups, rows, count, *refs):
-    (vol, k1, k2, k3, k4, fine_out, mid_out, low_out) = refs[:8]
-    (b_vol, b_one, b_pool, b_mid, t1, t2, t3, t4, send, recv, local) = refs[8:]
-    H, Z, W, C1, C2 = size
-    R, R2, RP = Z * C1, Z // 2 * C2, Z // 2 * C1
-    edges = Edges(groups, rows, count, send, recv)
-    load = pltpu.make_async_copy(vol, b_vol.at[pl.ds(R, H * R)], local)
-    load.start()
-    edges.greet()
-    load.wait()
-    edges.start(b_vol, H, R, 0)
-    band_kernel(t1, k1, C1, C1, C1, 0, Z)
-    conv_rows([(t1, b_vol, R)], into(b_one, R), H, R, lambda: edges.arrive(b_vol, H, R, 0))
-    edges.start(b_one, H, R, 1)
-    band_kernel(t2, k2, C1, C1, C1, 0, Z)
-    conv_rows([(t2, b_one, R)], plain(fine_out, R), H, R, lambda: edges.arrive(b_one, H, R, 1))
-    parts = halves(W)
-    for h in range(H // 2):
-        first, second = fine_out[2 * h * R : (2 * h + 1) * R, :], fine_out[(2 * h + 1) * R : (2 * h + 2) * R, :]
-        b_pool[(h + 1) * RP : (h + 2) * RP, :] = pool(first, second, C1, parts)
-    edges.start(b_pool, H // 2, RP, 2)
-    band_kernel(t3, k3, C2, C1, C1, 0, Z // 2)
-    conv_rows([(t3, b_pool, RP)], into(b_mid, R2), H // 2, R2, lambda: edges.arrive(b_pool, H // 2, RP, 2))
-    edges.start(b_mid, H // 2, R2, 3)
-    band_kernel(t4, k4, C2, C2, C2, 0, Z // 2)
-    conv_rows([(t4, b_mid, R2)], plain(mid_out, R2), H // 2, R2, lambda: edges.arrive(b_mid, H // 2, R2, 3))
-    parts = halves(W // 2)
-    R3 = R2 // 2
-    for h in range(H // 4):
-        first, second = mid_out[2 * h * R2 : (2 * h + 1) * R2, :], mid_out[(2 * h + 1) * R2 : (2 * h + 2) * R2, :]
-        low_out[h * R3 : (h + 1) * R3, :] = pool(first, second, C2, parts)
-    edges.sent(b_vol, H, R, 0)
-    edges.sent(b_one, H, R, 1)
-    edges.sent(b_pool, H // 2, RP, 2)
-    edges.sent(b_mid, H // 2, R2, 3)
-
-
-def decoder(size, groups, rows, count, *refs):
-    (fine, mid, low, whole, ub, mm, mr, um, fm, fr, out) = refs[:11]
-    (b_fine, b_mid, b_low, b_bot, bot, b_lift, b_three, four, b_raise, b_last) = refs[11:21]
-    (kt, t1, t2, t3a, t3b, t4, t5a, t5b, t6, send, recv, local) = refs[21:]
+def network(size, groups, rows, count, *refs):
+    (vol, b2, b1, k1, k2, k3, k4, ub, mm, mr, um, fm, fr, out) = refs[:14]
+    (b_vol, b_one, b_pool, b_first, e1, e2, e3, e4) = refs[14:22]
+    (b_fine, b_mid, b_low, b_bot, bot, b_lift, b_three, four, b_raise, b_last) = refs[22:32]
+    (kt, t1, t2, t3a, t3b, t4, t5a, t5b, t6, whole) = refs[32:42]
+    (send, recv, ring_send, ring_recv, side_send, side_recv, local) = refs[42:]
     H, Z, W, C1, C2, C3 = size
     R, R2, RP, RB = Z * C1, Z // 2 * C2, Z // 4 * C2, Z // 4 * C3
+    RQ = Z // 2 * C1
     H2, H4 = H // 2, H // 4
+    side = C3 // C2
+    each = -(-27 // side)
     edges = Edges(groups, rows, count, send, recv)
+    ring = Ring(edges, whole, ring_send, ring_recv, side_send, side_recv)
     loads = [
-        pltpu.make_async_copy(low, b_low.at[pl.ds(RP, H4 * RP)], local.at[0]),
-        pltpu.make_async_copy(mid, b_mid.at[pl.ds(R2, H2 * R2)], local.at[1]),
-        pltpu.make_async_copy(fine, b_fine.at[pl.ds(R, H * R)], local.at[2]),
+        pltpu.make_async_copy(vol, b_vol.at[pl.ds(R, H * R)], local.at[0]),
+        pltpu.make_async_copy(b2, whole.at[edges.me, pl.ds(0, 27)], local.at[1]),
     ]
     for load in loads:
         load.start()
-    edges.greet()
+    for t in range(each):
+        taps = [b1[q * each + t] if q * each + t < 27 else jnp.zeros(b1.shape[1:], bf16) for q in range(side)]
+        whole[edges.me, 27 + t] = jnp.concatenate(taps, axis=-1)
+    edges.greet(ring.neighbours())
     loads[0].wait()
+    edges.start(b_vol, H, R, 8)
+    loads[1].wait()
+    ring.step(0)
+    band_kernel(e1, k1, C1, C1, C1, 0, Z)
+    conv_rows([(e1, b_vol, R)], into(b_one, R), H, R, lambda: edges.arrive(b_vol, H, R, 8), lambda: ring.step(1))
+    edges.start(b_one, H, R, 9)
+    ring.step(2)
+    band_kernel(e2, k2, C1, C1, C1, 0, Z)
+    conv_rows([(e2, b_one, R)], into(b_fine, R), H, R, lambda: edges.arrive(b_one, H, R, 9), lambda: ring.step(3))
+    parts = halves(W)
+    for h in range(H2):
+        first, second = b_fine[(2 * h + 1) * R : (2 * h + 2) * R, :], b_fine[(2 * h + 2) * R : (2 * h + 3) * R, :]
+        b_pool[(h + 1) * RQ : (h + 2) * RQ, :] = pool(first, second, C1, parts)
+    edges.start(b_pool, H2, RQ, 10)
+    ring.step(4)
+    band_kernel(e3, k3, C2, C1, C1, 0, Z // 2, True)
+    conv_rows([(e3, b_pool, RQ)], into(b_first, R2), H2, R2, lambda: edges.arrive(b_pool, H2, RQ, 10), lambda: ring.step(5))
+    edges.start(b_first, H2, R2, 11)
+    ring.step(6)
+    band_kernel(e4, k4, C2, C2, C2, 0, Z // 2)
+    conv_rows([(e4, b_first, R2)], into(b_mid, R2), H2, R2, lambda: edges.arrive(b_first, H2, R2, 11))
+    parts = halves(W // 2)
+    for h in range(H4):
+        first, second = b_mid[(2 * h + 1) * R2 : (2 * h + 2) * R2, :], b_mid[(2 * h + 2) * R2 : (2 * h + 3) * R2, :]
+        b_low[(h + 1) * RP : (h + 2) * RP, :] = pool(first, second, C2, parts)
     edges.start(b_low, H4, RP, 0)
-    loads[1].wait()
+    ring.finish(7)
     edges.start(b_mid, H2, R2, 1)
-    loads[2].wait()
     edges.start(b_fine, H, R, 2)
-    side = C3 // C2
-    each = -(-27 // side)
     wide = Z // 4 * C2
     shape = (C3, side * wide)
     picks = one_hot(iota(shape, 0) == iota(shape, 1) // wide * C2 + (iota(shape, 1) & (C2 - 1)))
@@ -347,9 +432,11 @@
     band_kernel(t6, fr, C1, C1, C1, 0, Z)
     conv_rows([(t6, b_last, R)], plain(out, R), H, R, lambda: edges.arrive(b_last, H, R, 7))
     for at, (buf, height, cells) in enumerate(
-        [(b_low, H4, RP), (b_mid, H2, R2), (b_fine, H, R), (b_bot, H4, RB), (b_lift, H2, R2), (b_three, H2, R2), (b_raise, H, R), (b_last, H, R)]
+        [(b_low, H4, RP), (b_mid, H2, R2), (b_fine, H, R), (b_bot, H4, RB), (b_lift, H2, R2), (b_three, H2, R2), (b_raise, H, R), (b_last, H, R),
+         (b_vol, H, R), (b_one, H, R), (b_pool, H2, RQ), (b_first, H2, R2)]
     ):
         edges.sent(buf, height, cells, at)
+    ring.sent()
 
 
 def per_device(count, *args):
@@ -360,46 +447,33 @@
     R, R2, RP, RL, RB = Z * C1, Z // 2 * C2, Z // 2 * C1, Z // 4 * C2, Z // 4 * C3
     H2, H4, W2, W4 = H // 2, H // 4, W // 2, W // 4
     flat = lambda k: k.reshape(-1, k.shape[-1])
-    side = C3 // C2
-    each = -(-27 // side)
-    first = jnp.pad(b1.reshape(27, own, C2), ((0, each * side - 27), (0, 0), (0, 0))).reshape(side, each, own, C2)
-    first = jnp.concatenate([first[q] for q in range(side)], axis=-1)
-    packed = jnp.concatenate([b2.reshape(27, own, C3), first], axis=0)
-    whole = lax.all_gather(packed, "rows", axis=0)
+    each = -(-27 // (C3 // C2))
+    taps = 27 + each + (27 + each) % 2
+    chips = count // 2
     cells = volume.transpose(1, 2, 0, 3).reshape(H * R, W)
     vmem, hbm = pl.BlockSpec(memory_space=pltpu.VMEM), pl.BlockSpec(memory_space=pl.ANY)
-    V = lambda r, c: pltpu.VMEM((r, c), bf16)
+    V = lambda *shape: pltpu.VMEM(shape, bf16)
     D = pltpu.SemaphoreType.DMA
-    fine, mid, low = pl.pallas_call(
-        functools.partial(encoder, (H, Z, W, C1, C2), "groups", "rows", count),
-        out_shape=[jax.ShapeDtypeStruct(s, bf16) for s in ((H * R, W), (H2 * R2, W2), (H4 * RL, W4))],
-        in_specs=[hbm] + [vmem] * 4,
-        out_specs=[vmem] * 3,
+    out = pl.pallas_call(
+        functools.partial(network, (H, Z, W, C1, C2, C3), "groups", "rows", count),
+        out_shape=jax.ShapeDtypeStruct((H * R, W), bf16),
+        in_specs=[hbm] * 2 + [vmem] * 11,
+        out_specs=vmem,
         scratch_shapes=[
             V((H + 2) * R, W), V((H + 2) * R, W), V((H2 + 2) * RP, W2), V((H2 + 2) * R2, W2),
             V(3 * R, 3 * R), V(3 * R, 3 * R), V(3 * R2, 3 * RP), V(3 * R2, 3 * R2),
-            D((4, 2)), D((4, 2)), D,
-        ],
-        compiler_params=pltpu.CompilerParams(collective_id=0, has_side_effects=True, vmem_limit_bytes=VMEM_LIMIT),
-        cost_estimate=pl.CostEstimate(flops=10**10, bytes_accessed=10**8, transcendentals=0),
-        name="encoder",
-    )(cells, flat(f1), flat(f2), flat(m1), flat(m2))
-    out = pl.pallas_call(
-        functools.partial(decoder, (H, Z, W, C1, C2, C3), "groups", "rows", count),
-        out_shape=jax.ShapeDtypeStruct((H * R, W), bf16),
-        in_specs=[hbm] * 3 + [vmem] * 7,
-        out_specs=vmem,
-        scratch_shapes=[
             V((H + 2) * R, W), V((H2 + 2) * R2, W2), V((H4 + 2) * RL, W4), V((H4 + 2) * RB, W4), V(H4 * RB, W4),
             V((H2 + 2) * R2, W2), V((H2 + 2) * R2, W2), V(H2 * R2, W2), V((H + 2) * R, W), V((H + 2) * R, W),
             V(27 * C3, Z // 4 * C2), V(3 * RB, 3 * RL), V(3 * RB, 3 * RB), V(3 * R2, 3 * R2), V(3 * R2, 3 * R2),
-            V(3 * R2, 3 * R2), V(3 * R, 3 * R), V(3 * R, 3 * R), V(3 * R, 3 * R),
-            D((8, 2)), D((8, 2)), D((3,)),
+            V(3 * R2, 3 * R2), V(3 * R, 3 * R), V(3 * R, 3 * R), V(3 * R, 3 * R), V(count, taps, own, C3),
+            D((12, 2)), D((12, 2)), D((chips - 1, 2)), D((chips - 1, 2)), D((chips, 2)), D((chips, 2)), D((2,)),
         ],
-        compiler_params=pltpu.CompilerParams(collective_id=1, has_side_effects=True, vmem_limit_bytes=VMEM_LIMIT),
-        cost_estimate=pl.CostEstimate(flops=10**10, bytes_accessed=10**8, transcendentals=0),
-        name="decoder",
-    )(fine, mid, low, whole, flat(ub), flat(mm), flat(mr), flat(um), flat(fm), flat(fr))
+        compiler_params=pltpu.CompilerParams(collective_id=0, has_side_effects=True, vmem_limit_bytes=VMEM_LIMIT),
+        name="network",
+    )(
+        cells, b2.reshape(27, own, C3), b1.reshape(27, own, C2), flat(f1), flat(f2), flat(m1.swapaxes(3, 4)), flat(m2),
+        flat(ub), flat(mm), flat(mr), flat(um), flat(fm), flat(fr),
+    )
     return out.reshape(H, Z, C1, W).transpose(2, 0, 1, 3)
 
 

time: 128 us -> 101 us (0.79); the launches traced: 126 us -> 101 us
  waiting for transfers between devices: 14.5 us -> 0 us
  between operations: 13.4 us -> 0.01 us
  Pallas kernels: 88.2 us -> 95.5 us
  local copies, waits for them, and re-layouts: 8.27 us -> 5.55 us
  other arithmetic: 1.76 us -> 0 us
    all_gather x1 -> x0, waiting for transfers between devices: 14.5 us -> none  [per_device(): whole = lax.all_gather(packed, 'rows', axis=0)]
    pallas_call x2 -> x1, Pallas kernels: 88.2 us -> 95.5 us  [per_device(): pl.pallas_call(functools.partial(network, (H, Z, W, C1, C2, C3), 'groups'...]
    unnamed x1 -> x0, local copies, waits for them, and re-layouts: 1.91 us -> none
    concatenate x1 -> x0, other arithmetic: 1.76 us -> none  [per_device(): packed = jnp.concatenate([b2.reshape(27, own, C3), first], axis=0)]
  transfers between devices with their start and end apart: 1 -> 0, of which waited for: 1 -> 0; matrix products, arithmetic and copies ran while one was open for 4% -> 0% of each run, Pallas kernels for 31% -> 0%
where the time goes in v1:
time: 101 us
  Pallas kernels  95.5 us (95%)
  local copies, waits for them, and re-layouts  5.55 us (5%)
    pallas_call x1, Pallas kernels, per_device(): pl.pallas_call(functools.partial(network, (H, Z, W, C1, C2, C3), 'groups'...  95.5 us
    reshape x1, local copies, waits for them, and re-layouts, per_device(): return out.reshape(H, Z, C1, W).transpose(2, 0, 1, 3)  2.77 us
    transpose x1, local copies, waits for them, and re-layouts, per_device(): cells = volume.transpose(1, 2, 0, 3).reshape(H * R, W)  2.77 us

profile of v1, /device:TPU:9, one launch (start us, length us, event | category | flops | bytes accessed | tf_op | source)
XLA Modules:
  0.0 101.0 jit_solution(18273262890582412092)
XLA Ops:
  0.0 2.8 %copy.14 = bf16[4,8,32,512]{3,2,1,0:T(8,128)(2,1)} copy(bf16[4,8,32,512]{3,1,0,2:T(8,128)(2,1)} %bitcast.22) | data formatting | bytes 2097152 | tf_op jit(solution)/shard_map/transpose | solution.py:453
  2.8 95.5 %network.1 = bf16[1024,512]{1,0:T(8,128)(2,1)} custom-call(bf16[1024,512]{1,0:T(8,128)(2,1)} %bitcast.21, bf16[27,16,256]{2,1,0:T(8,128)(2,1)} %bitcast.27, bf16[27,16,64]{2,1,0:T(8,128)(2,1)} %bitcast.33, bf16[864,32]{1,0:T(8,128)(2,1)} %bitcast.28, bf16[864,32]{1,0:T(8,128)(2,1)} %bitcast.29, bf16[864,64]{1,0:T(8,128)(2,1)} %bitcast.30, ...), custom_call_target="tpu_custom_call" | custom-call | tf_op jit(solution)/shard_map/network/pallas_call | solution.py:457
  98.2 2.8 %copy.17 = bf16[4,8,32,512]{3,1,0,2:T(8,128)(2,1)} copy(bf16[4,8,32,512]{3,2,1,0:T(8,128)(2,1)} %bitcast.20) | data formatting | bytes 2097152 | tf_op jit(solution)/shard_map/reshape | solution.py:477

commit v2 on v1

--- a/solution.py
+++ b/solution.py
@@ -62,17 +62,23 @@
     lane = iota((count, width), 1)
     left = jnp.where(lane == 0, 0.0, pltpu.roll(sums[:count], 1, 1))
     right = jnp.where(lane == width - 1, 0.0, pltpu.roll(sums[2 * count :], width - 1, 1))
-    total = left + sums[count : 2 * count] + right
+    return left + sums[count : 2 * count] + right
+
+
+def leaky(total):
     return jnp.maximum(total, leakage * total).astype(bf16)
 
 
-def conv_rows(sources, store, height, count, arrive, before=lambda: None):
+def conv_rows(sources, store, height, count, arrive, before=lambda: None, held=None, last=leaky):
     def row(at):
         sums = None
         for banded, rows, cells in sources:
             part = dot(banded[...], rows[pl.ds(pl.multiple_of(at * cells, cells), 3 * cells), :])
             sums = part if sums is None else sums + part
-        store(at, finish(sums, count))
+        total = finish(sums, count)
+        if held is not None:
+            total = total + held[pl.ds(pl.multiple_of(at * count, count), count), :]
+        store(at, last(total))
 
     if height > 2:
 
@@ -314,8 +320,8 @@
     (vol, b2, b1, k1, k2, k3, k4, ub, mm, mr, um, fm, fr, out) = refs[:14]
     (b_vol, b_one, b_pool, b_first, e1, e2, e3, e4) = refs[14:22]
     (b_fine, b_mid, b_low, b_bot, bot, b_lift, b_three, four, b_raise, b_last) = refs[22:32]
-    (kt, t1, t2, t3a, t3b, t4, t5a, t5b, t6, whole) = refs[32:42]
-    (send, recv, ring_send, ring_recv, side_send, side_recv, local) = refs[42:]
+    (kt, t1, t2, t3a, t3b, t4, t5a, t5b, t6, whole, fine_part, mid_part) = refs[32:44]
+    (send, recv, ring_send, ring_recv, side_send, side_recv, local) = refs[44:]
     H, Z, W, C1, C2, C3 = size
     R, R2, RP, RB = Z * C1, Z // 2 * C2, Z // 4 * C2, Z // 4 * C3
     RQ = Z // 2 * C1
@@ -351,9 +357,9 @@
     edges.start(b_pool, H2, RQ, 10)
     ring.step(4)
     band_kernel(e3, k3, C2, C1, C1, 0, Z // 2, True)
-    conv_rows([(e3, b_pool, RQ)], into(b_first, R2), H2, R2, lambda: edges.arrive(b_pool, H2, RQ, 10), lambda: ring.step(5))
+    conv_rows([(e3, b_pool, RQ)], into(b_first, R2), H2, R2, lambda: edges.arrive(b_pool, H2, RQ, 10))
     edges.start(b_first, H2, R2, 11)
-    ring.step(6)
+    ring.step(5)
     band_kernel(e4, k4, C2, C2, C2, 0, Z // 2)
     conv_rows([(e4, b_first, R2)], into(b_mid, R2), H2, R2, lambda: edges.arrive(b_first, H2, R2, 11))
     parts = halves(W // 2)
@@ -361,9 +367,19 @@
         first, second = b_mid[(2 * h + 1) * R2 : (2 * h + 2) * R2, :], b_mid[(2 * h + 2) * R2 : (2 * h + 3) * R2, :]
         b_low[(h + 1) * RP : (h + 2) * RP, :] = pool(first, second, C2, parts)
     edges.start(b_low, H4, RP, 0)
-    ring.finish(7)
     edges.start(b_mid, H2, R2, 1)
     edges.start(b_fine, H, R, 2)
+    ring.step(6)
+    band_kernel(t5a, fm, C1, 2 * C1, C1, 0, Z)
+    conv_rows([(t5a, b_fine, R)], plain(fine_part, R), H, R, lambda: edges.arrive(b_fine, H, R, 2), last=lambda total: total)
+    ring.step(7)
+    band_kernel(t3a, mm, C2, 2 * C2, C2, 0, Z // 2)
+    conv_rows([(t3a, b_mid, R2)], plain(mid_part, R2), H2, R2, lambda: edges.arrive(b_mid, H2, R2, 1), last=lambda total: total)
+    band_kernel(t3b, mm, C2, 2 * C2, C2, C2, Z // 2)
+    band_kernel(t4, mr, C2, C2, C2, 0, Z // 2)
+    band_kernel(t5b, fm, C1, 2 * C1, C1, C1, Z)
+    band_kernel(t6, fr, C1, C1, C1, 0, Z)
+    ring.finish(8)
     wide = Z // 4 * C2
     shape = (C3, side * wide)
     picks = one_hot(iota(shape, 0) == iota(shape, 1) // wide * C2 + (iota(shape, 1) & (C2 - 1)))
@@ -400,16 +416,8 @@
 
         lift(bot[h * RB : (h + 1) * RB, :], ub, C3, C2, woven, store)
     edges.start(b_lift, H2, R2, 4)
-    band_kernel(t3a, mm, C2, 2 * C2, C2, 0, Z // 2)
-    band_kernel(t3b, mm, C2, 2 * C2, C2, C2, Z // 2)
-
-    def both():
-        edges.arrive(b_mid, H2, R2, 1)
-        edges.arrive(b_lift, H2, R2, 4)
-
-    conv_rows([(t3a, b_mid, R2), (t3b, b_lift, R2)], into(b_three, R2), H2, R2, both)
+    conv_rows([(t3b, b_lift, R2)], into(b_three, R2), H2, R2, lambda: edges.arrive(b_lift, H2, R2, 4), held=mid_part)
     edges.start(b_three, H2, R2, 5)
-    band_kernel(t4, mr, C2, C2, C2, 0, Z // 2)
     conv_rows([(t4, b_three, R2)], plain(four, R2), H2, R2, lambda: edges.arrive(b_three, H2, R2, 5))
     woven = weave(W)
     for h in range(H2):
@@ -420,16 +428,8 @@
 
         lift(four[h * R2 : (h + 1) * R2, :], um, C2, C1, woven, store)
     edges.start(b_raise, H, R, 6)
-    band_kernel(t5a, fm, C1, 2 * C1, C1, 0, Z)
-    band_kernel(t5b, fm, C1, 2 * C1, C1, C1, Z)
-
-    def last():
-        edges.arrive(b_fine, H, R, 2)
-        edges.arrive(b_raise, H, R, 6)
-
-    conv_rows([(t5a, b_fine, R), (t5b, b_raise, R)], into(b_last, R), H, R, last)
+    conv_rows([(t5b, b_raise, R)], into(b_last, R), H, R, lambda: edges.arrive(b_raise, H, R, 6), held=fine_part)
     edges.start(b_last, H, R, 7)
-    band_kernel(t6, fr, C1, C1, C1, 0, Z)
     conv_rows([(t6, b_last, R)], plain(out, R), H, R, lambda: edges.arrive(b_last, H, R, 7))
     for at, (buf, height, cells) in enumerate(
         [(b_low, H4, RP), (b_mid, H2, R2), (b_fine, H, R), (b_bot, H4, RB), (b_lift, H2, R2), (b_three, H2, R2), (b_raise, H, R), (b_last, H, R),
@@ -466,6 +466,7 @@
             V((H2 + 2) * R2, W2), V((H2 + 2) * R2, W2), V(H2 * R2, W2), V((H + 2) * R, W), V((H + 2) * R, W),
             V(27 * C3, Z // 4 * C2), V(3 * RB, 3 * RL), V(3 * RB, 3 * RB), V(3 * R2, 3 * R2), V(3 * R2, 3 * R2),
             V(3 * R2, 3 * R2), V(3 * R, 3 * R), V(3 * R, 3 * R), V(3 * R, 3 * R), V(count, taps, own, C3),
+            pltpu.VMEM((H * R, W), f32), pltpu.VMEM((H2 * R2, W2), f32),
             D((12, 2)), D((12, 2)), D((chips - 1, 2)), D((chips - 1, 2)), D((chips, 2)), D((chips, 2)), D((2,)),
         ],
         compiler_params=pltpu.CompilerParams(collective_id=0, has_side_effects=True, vmem_limit_bytes=VMEM_LIMIT),

time: 101 us -> 102 us (level); the launches traced: 101 us -> 99.8 us
  Pallas kernels: 95.5 us -> 94.2 us
    pallas_call x1, Pallas kernels: 95.5 us -> 94.2 us  [per_device(): pl.pallas_call(functools.partial(network, (H, Z, W, C1, C2, C3), 'groups'...]
where the time goes in v2:
time: 102 us; the launch traced here: 99.8 us
  Pallas kernels  94.2 us (92%)
  local copies, waits for them, and re-layouts  5.55 us (5%)
    pallas_call x1, Pallas kernels, per_device(): pl.pallas_call(functools.partial(network, (H, Z, W, C1, C2, C3), 'groups'...  94.2 us
    reshape x1, local copies, waits for them, and re-layouts, per_device(): return out.reshape(H, Z, C1, W).transpose(2, 0, 1, 3)  2.77 us
    transpose x1, local copies, waits for them, and re-layouts, per_device(): cells = volume.transpose(1, 2, 0, 3).reshape(H * R, W)  2.77 us

profile of v2, /device:TPU:9, one launch (start us, length us, event | category | flops | bytes accessed | tf_op | source)
XLA Modules:
  0.0 99.8 jit_solution(4727111451783890163)
XLA Ops:
  0.0 2.8 %copy.14 = bf16[4,8,32,512]{3,2,1,0:T(8,128)(2,1)} copy(bf16[4,8,32,512]{3,1,0,2:T(8,128)(2,1)} %bitcast.22) | data formatting | bytes 2097152 | tf_op jit(solution)/shard_map/transpose | solution.py:453
  2.8 94.2 %network.1 = bf16[1024,512]{1,0:T(8,128)(2,1)} custom-call(bf16[1024,512]{1,0:T(8,128)(2,1)} %bitcast.21, bf16[27,16,256]{2,1,0:T(8,128)(2,1)} %bitcast.27, bf16[27,16,64]{2,1,0:T(8,128)(2,1)} %bitcast.33, bf16[864,32]{1,0:T(8,128)(2,1)} %bitcast.28, bf16[864,32]{1,0:T(8,128)(2,1)} %bitcast.29, bf16[864,64]{1,0:T(8,128)(2,1)} %bitcast.30, ...), custom_call_target="tpu_custom_call" | custom-call | tf_op jit(solution)/shard_map/network/pallas_call | solution.py:457
  97.0 2.8 %copy.17 = bf16[4,8,32,512]{3,1,0,2:T(8,128)(2,1)} copy(bf16[4,8,32,512]{3,2,1,0:T(8,128)(2,1)} %bitcast.20) | data formatting | bytes 2097152 | tf_op jit(solution)/shard_map/reshape | solution.py:478

commit v3 on v2

--- a/solution.py
+++ b/solution.py
@@ -357,9 +357,9 @@
     edges.start(b_pool, H2, RQ, 10)
     ring.step(4)
     band_kernel(e3, k3, C2, C1, C1, 0, Z // 2, True)
-    conv_rows([(e3, b_pool, RQ)], into(b_first, R2), H2, R2, lambda: edges.arrive(b_pool, H2, RQ, 10))
+    conv_rows([(e3, b_pool, RQ)], into(b_first, R2), H2, R2, lambda: edges.arrive(b_pool, H2, RQ, 10), lambda: ring.step(5))
     edges.start(b_first, H2, R2, 11)
-    ring.step(5)
+    ring.step(6)
     band_kernel(e4, k4, C2, C2, C2, 0, Z // 2)
     conv_rows([(e4, b_first, R2)], into(b_mid, R2), H2, R2, lambda: edges.arrive(b_first, H2, R2, 11))
     parts = halves(W // 2)
@@ -369,10 +369,8 @@
     edges.start(b_low, H4, RP, 0)
     edges.start(b_mid, H2, R2, 1)
     edges.start(b_fine, H, R, 2)
-    ring.step(6)
     band_kernel(t5a, fm, C1, 2 * C1, C1, 0, Z)
-    conv_rows([(t5a, b_fine, R)], plain(fine_part, R), H, R, lambda: edges.arrive(b_fine, H, R, 2), last=lambda total: total)
-    ring.step(7)
+    conv_rows([(t5a, b_fine, R)], plain(fine_part, R), H, R, lambda: edges.arrive(b_fine, H, R, 2), lambda: ring.step(7), last=lambda total: total)
     band_kernel(t3a, mm, C2, 2 * C2, C2, 0, Z // 2)
     conv_rows([(t3a, b_mid, R2)], plain(mid_part, R2), H2, R2, lambda: edges.arrive(b_mid, H2, R2, 1), last=lambda total: total)
     band_kernel(t3b, mm, C2, 2 * C2, C2, C2, Z // 2)

time: 102 us -> 103 us (level)
  Pallas kernels: 94.2 us -> 95.4 us
    pallas_call x1, Pallas kernels: 94.2 us -> 95.4 us  [per_device(): pl.pallas_call(functools.partial(network, (H, Z, W, C1, C2, C3), 'groups'...]
where the time goes in v3:
time: 103 us; the launch traced here: 101 us
  Pallas kernels  95.4 us (93%)
  local copies, waits for them, and re-layouts  5.55 us (5%)
    pallas_call x1, Pallas kernels, per_device(): pl.pallas_call(functools.partial(network, (H, Z, W, C1, C2, C3), 'groups'...  95.4 us
    reshape x1, local copies, waits for them, and re-layouts, per_device(): return out.reshape(H, Z, C1, W).transpose(2, 0, 1, 3)  2.77 us
    transpose x1, local copies, waits for them, and re-layouts, per_device(): cells = volume.transpose(1, 2, 0, 3).reshape(H * R, W)  2.77 us

profile of v3, /device:TPU:9, one launch (start us, length us, event | category | flops | bytes accessed | tf_op | source)
XLA Modules:
  0.0 101.0 jit_solution(12843470324744152913)
XLA Ops:
  0.0 2.8 %copy.14 = bf16[4,8,32,512]{3,2,1,0:T(8,128)(2,1)} copy(bf16[4,8,32,512]{3,1,0,2:T(8,128)(2,1)} %bitcast.22) | data formatting | bytes 2097152 | tf_op jit(solution)/shard_map/transpose | solution.py:451
  2.8 95.4 %network.1 = bf16[1024,512]{1,0:T(8,128)(2,1)} custom-call(bf16[1024,512]{1,0:T(8,128)(2,1)} %bitcast.21, bf16[27,16,256]{2,1,0:T(8,128)(2,1)} %bitcast.27, bf16[27,16,64]{2,1,0:T(8,128)(2,1)} %bitcast.33, bf16[864,32]{1,0:T(8,128)(2,1)} %bitcast.28, bf16[864,32]{1,0:T(8,128)(2,1)} %bitcast.29, bf16[864,64]{1,0:T(8,128)(2,1)} %bitcast.30, ...), custom_call_target="tpu_custom_call" | custom-call | tf_op jit(solution)/shard_map/network/pallas_call | solution.py:455
  98.2 2.8 %copy.17 = bf16[4,8,32,512]{3,1,0,2:T(8,128)(2,1)} copy(bf16[4,8,32,512]{3,2,1,0:T(8,128)(2,1)} %bitcast.20) | data formatting | bytes 2097152 | tf_op jit(solution)/shard_map/reshape | solution.py:476
